TPU v7x, 32 devices: a whole 2x2x4 slice. The times are simulated.
32 devices in a mesh: tm: 2 (over x), band: 16 (over z, y, core).
Axes of the slice: x: 2, y: 2, z: 4, core: 2. Of those that a mesh axis runs over, the one named last changes fastest.
Arguments:
- samples: bfloat16 [512, 256, 2, 512], P('tm', 'band'), may hold values from -6 to 6
- weights: bfloat16 [256, 2, 512, 512], P('band', None, None, 'tm'), may hold values from -0.25 to 0.25
- prototype: float32 [1024], replicated, may hold values from 0.25 to 1
Outputs:
- beam_series: float32 [512, 131072], P('band', 'tm')
All inputs are finite; a program needn't handle non-finite values.
Results may differ from a plain program's by a relative error of at most 0.004.
Values may be sent and summed in bfloat16 or wider, within the bound.
A program may use at most 128 MiB of HBM per device.

v0:
```python
import math

import jax
import jax.numpy as jnp
from jax import lax
from jax.sharding import PartitionSpec as P

M = 512
K = 256
FIRST_BIN = 32


def passed_along(block, axis, distance):
    devices = range(lax.axis_size(axis))
    route = [(i - distance, i) for i in devices if i - distance in devices]
    return lax.ppermute(block, axis, route)


def synth_table(prototype):
    length = prototype.shape[0]
    bin_index = jnp.arange(K, dtype=jnp.int32) + FIRST_BIN
    tap_index = jnp.arange(length, dtype=jnp.int32)
    phase_index = bin_index[:, None] * tap_index[None, :] % M
    angles = phase_index.astype(jnp.float32) * (2.0 * math.pi / M)
    scaled = prototype[None, :] / math.sqrt(K)
    window_table = jnp.stack([jnp.cos(angles) * scaled, -jnp.sin(angles) * scaled], axis=1)
    return window_table.astype(jnp.bfloat16)


def intersection_add(frames, hop_size):
    pieces = frames.shape[-1] // hop_size
    pieces_view = frames.reshape(frames.shape[:-1] + (pieces, hop_size))
    leading = [(0, 0)] * (pieces_view.ndim - 3)
    intersection = jnp.zeros(
        pieces_view.shape[:-3] + (pieces_view.shape[-3] + pieces - 1, hop_size), frames.dtype
    )
    for lag in range(pieces):
        intersection = intersection + jnp.pad(
            pieces_view[..., lag, :], leading + [(lag, pieces - 1 - lag), (0, 0)]
        )
    return intersection


def beam_form(samples, weights):
    products = jnp.einsum("fkce,kdeb->bkdcf", samples, weights, preferred_element_type=jnp.float32)
    real_part = products[:, :, 0, 0] + products[:, :, 1, 1]
    imag_part = products[:, :, 0, 1] - products[:, :, 1, 0]
    return jnp.stack([real_part, imag_part], axis=2).astype(jnp.bfloat16)


def synthesize(spectra, window_table):
    return jnp.einsum("bkcf,kcn->bfn", spectra, window_table, preferred_element_type=jnp.float32)


def shards(samples, weights, prototype):
    hop_size = M // 2
    beam_parts = beam_form(samples, lax.all_gather(weights, "tm", axis=3, tiled=True))
    gathered = lax.all_to_all(beam_parts, "band", split_axis=0, concat_axis=1, tiled=True)
    window_table = synth_table(prototype)
    frame_total = gathered.shape[3]
    tail_rows = prototype.shape[0] // hop_size - 1
    frames = synthesize(gathered, window_table)
    summed = intersection_add(frames, hop_size)
    prev_tail = passed_along(summed[:, frame_total:], "tm", 1)
    block_out = summed[:, :frame_total]
    block_out = jnp.concatenate(
        [block_out[:, :tail_rows] + prev_tail, block_out[:, tail_rows:]], axis=1
    )
    return block_out.reshape(block_out.shape[0], frame_total * hop_size)


def solution(mesh):
    in_specs = (P("tm", "band", None, None), P("band", None, None, "tm"), P())
    out_specs = P("band", "tm")
    return jax.shard_map(shards, mesh=mesh, in_specs=in_specs, out_specs=out_specs, check_vma=False)
```

profile of v0, /device:TPU:14, one launch (start us, length us, event | category | flops | bytes accessed | tf_op | source)
XLA Modules:
  0.0 549.9 jit_solution(13992426558295163922)
XLA Ops:
  6.5 0.0 all-gather.2.cloned.1.call-start
  6.5 12.3 %copy.32 = bf16[16,2,512,256]{2,3,1,0:T(8,128)(2,1)} copy(bf16[16,2,512,256]{3,2,1,0:T(8,128)(2,1)} %param.4) | data formatting | bytes 16777216 | tf_op args[1]
  18.8 0.0 all-gather.2.cloned.1.call-update
  18.8 199.2 %all-gather.2.cloned.1.call-done = bf16[16,2,512,512]{2,3,1,0:T(8,128)(2,1)} async-done(((bf16[16,2,512,256]{2,3,1,0:T(8,128)(2,1)}), bf16[16,2,512,512]{2,3,1,0:T(8,128)(2,1)}) %all-gather.2.cloned.1.call-update) | async-done | bytes 16777232 | tf_op jit(solution)/shard_map/all_gather | solution.py:57
  218.0 27.4 %fusion.2 = f32[512,16,2,2,256]{4,0,3,2,1:T(8,128)} fusion(bf16[16,2,512,512]{2,3,1,0:T(8,128)(2,1)} %all-gather.2.cloned.1.call-done, bf16[256,16,2,512,1]{3,2,1,0,4:T(2,128)(2,1)} %bitcast.63), kind=kOutput, calls=%fused_computation.2 | convolution fusion | flops 8589934592 | bytes 58720256 | tf_op jit(solution)/shard_map/fkce,kdeb->bkdcf/dot_general | solution.py:45
  245.4 6.6 %fusion.10 = bf16[512,16,1,256]{3,0,1,2:T(8,128)(2,1)S(1)} fusion(f32[512,16,2,2,256]{4,0,3,2,1:T(8,128)} %fusion.2), kind=kLoop, calls=%fused_computation.21 | loop fusion | flops 4194304 | bytes 20971520 | tf_op jit(solution)/shard_map/sub | solution.py:47
  252.0 8.5 %fusion.9 = bf16[512,16,1,256]{3,0,1,2:T(8,128)(2,1)} fusion(f32[512,16,2,2,256]{4,0,3,2,1:T(8,128)} %fusion.2), kind=kLoop, calls=%fused_computation.20 | loop fusion | flops 4194304 | bytes 20971520 | tf_op jit(solution)/shard_map/add | solution.py:46
  260.5 6.3 %pad_maximum_fusion = bf16[512,16,2,256]{3,0,1,2:T(8,128)(2,1)} fusion(bf16[512,16,1,256]{3,0,1,2:T(8,128)(2,1)S(1)} %fusion.10, bf16[512,16,1,256]{3,0,1,2:T(8,128)(2,1)} %fusion.9), kind=kLoop, calls=%fused_computation.17 | loop fusion | flops 4194304 | bytes 16777216 | tf_op jit(solution)/shard_map/stack | solution.py:48
  266.9 11.4 %copy.36 = bf16[512,16,2,256]{3,1,2,0:T(8,128)(2,1)} copy(bf16[512,16,2,256]{3,0,1,2:T(8,128)(2,1)} %pad_maximum_fusion) | data formatting | bytes 16777216 | tf_op jit(solution)/shard_map/stack | solution.py:48
  278.3 0.0 copy-start.1
  278.3 6.2 %all-to-all-start = ((bf16[512,16,2,256]{3,1,2,0:T(8,128)(2,1)}), bf16[512,16,2,256]{3,1,2,0:T(8,128)(2,1)}, u32[]{:S(2)}, u32[]{:S(2)}) async-start(bf16[512,16,2,256]{3,1,2,0:T(8,128)(2,1)} %copy.36), calls=%async_computation | async-start | bytes 16777216 | tf_op jit(solution)/shard_map/all_to_all | solution.py:58
  284.5 0.0 copy-done.1
  284.5 4.6 multiply_convert_fusion.1
  289.2 0.1 pad_maximum_fusion.2
  289.3 177.3 %all-to-all-done = bf16[512,16,2,256]{3,1,2,0:T(8,128)(2,1)} async-done(((bf16[512,16,2,256]{3,1,2,0:T(8,128)(2,1)}), bf16[512,16,2,256]{3,1,2,0:T(8,128)(2,1)}, u32[]{:S(2)}, u32[]{:S(2)}) %all-to-all-start) | async-done | bytes 8388640 | tf_op jit(solution)/shard_map/all_to_all | solution.py:58
  466.5 8.0 %copy.37 = bf16[32,16,16,2,256]{4,2,1,3,0:T(8,128)(2,1)} copy(bf16[32,16,16,2,256]{4,2,3,0,1:T(8,128)(2,1)} %bitcast.7) | data formatting | bytes 16777216 | tf_op jit(solution)/shard_map/all_to_all | solution.py:58
  474.6 18.7 %convolution_bitcast_fusion = f32[32,256,4,256]{3,1,2,0:T(8,128)} fusion(bf16[32,256,2,256,1]{3,1,2,4,0:T(8,128)(2,1)} %bitcast.64, bf16[4,256,2,256]{3,1,0,2:T(8,128)(2,1)S(1)} %bitcast.65), kind=kOutput, calls=%fused_computation.3 | convolution fusion | flops 8589934592 | bytes 42991616 | tf_op jit(solution)/shard_map/bkcf,kcn->bfn/dot_general | solution.py:52
  493.3 20.8 %slice_bitcast_fusion.3 = (f32[32,256,256]{2,1,0:T(8,128)S(1)}, f32[32,256,256]{2,1,0:T(8,128)}, f32[32,256,256]{2,1,0:T(8,128)}, f32[32,256,256]{2,1,0:T(8,128)}) fusion(f32[32,256,4,256]{3,1,2,0:T(8,128)} %convolution_bitcast_fusion), kind=kLoop, calls=%fused_computation.10 | loop fusion | bytes 67108864 | tf_op jit(solution)/shard_map/squeeze | solution.py:39
  514.0 1.2 pad_add_fusion.3
  515.2 1.3 collective-permute-start
  516.5 13.6 %pad_add_fusion = f32[32,253,256]{2,1,0:T(8,128)} fusion(f32[32,256,256]{2,1,0:T(8,128)} %get-tuple-element.7, f32[32,256,256]{2,1,0:T(8,128)} %get-tuple-element.8, f32[32,256,256]{2,1,0:T(8,128)} %get-tuple-element.6, f32[32,256,256]{2,1,0:T(8,128)S(1)} %get-tuple-element.5), kind=kLoop, calls=%fused_computation.4 | loop fusion | flops 6217728 | bytes 41844736 | tf_op jit(solution)/shard_map/add | solution.py:38
  530.1 0.0 copy-start
  530.1 0.0 collective-permute-done
  530.1 1.3 add_add_fusion
  531.4 2.3 copy-done
  533.6 1.2 pad_maximum_fusion.1
  534.8 8.3 %copy.56 = f32[4,8,256,256]{3,1,2,0:T(8,128)} copy(f32[4,8,256,256]{3,2,1,0:T(8,128)S(1)} %bitcast.62) | data formatting | bytes 16777216
  (2 shorter events, 0.0 us)
Async XLA Ops:
  6.5 211.5 %all-gather.2.cloned.1.call-start = ((), (), s32[]{:S(2)}) async-start(), calls=%async_computation.1 | async-start | bytes 25165824 | tf_op jit(solution)/shard_map/all_gather | solution.py:57
  278.3 6.2 %copy-start.1 = (f32[1024]{0:T(1024)S(1)}, f32[1024]{0:T(1024)}, u32[]{:S(2)}) copy-start(f32[1024]{0:T(1024)} %param.5) | copy-start | bytes 12292
  278.3 188.3 %all-to-all-start = ((bf16[512,16,2,256]{3,1,2,0:T(8,128)(2,1)}), bf16[512,16,2,256]{3,1,2,0:T(8,128)(2,1)}, u32[]{:S(2)}, u32[]{:S(2)}) async-start(bf16[512,16,2,256]{3,1,2,0:T(8,128)(2,1)} %copy.36), calls=%async_computation | async-start | bytes 16777216 | tf_op jit(solution)/shard_map/all_to_all | solution.py:58
  515.2 14.9 %collective-permute-start = (f32[32,3,256]{2,1,0:T(4,128)S(1)}, f32[32,3,256]{2,1,0:T(4,128)S(1)}, u32[]{:S(2)}, u32[]{:S(2)}) collective-permute-start(f32[32,3,256]{2,1,0:T(4,128)S(1)} %pad_add_fusion.3), channel_id=1, source_target_pairs={{0,16},{1,17},{2,18},{3,19},{4,20},{5,21},{6,22},{7,23},{8,24},{9,... | collective-permute-start | bytes 294920 | tf_op jit(solution)/shard_map/ppermute | solution.py:16
  530.1 3.5 copy-start
Sparse Core Ops, SparseCore 0:
  19.0 199.0 all-gather.1
where the time goes:
time: 553 us; the launch traced here: 550 us
  waiting for transfers between devices  376 us (68%)
  local copies, waits for them, and re-layouts  63 us (11%)
  matrix products  46.1 us (8%)
  other arithmetic  43.4 us (8%)
  between operations  13.5 us (2%)
  starting transfers between devices  7.51 us (1%)
    all_gather x1, waiting for transfers between devices, shards(): lax.all_gather(weights, 'tm', axis=3, tiled=True)  199 us
    all_to_all x1, waiting for transfers between devices, shards(): lax.all_to_all(beam_parts, 'band', split_axis=0, concat_axis=1, tiled=True)  177 us
    dot_general x1, matrix products, beam_form(): jnp.einsum('fkce,kdeb->bkdcf', samples, weights, preferred_element_type=j...  27.4 us
    unnamed x6, local copies, waits for them, and re-layouts  22.8 us
    squeeze x1, local copies, waits for them, and re-layouts, intersection_add(): pieces_view[..., lag, :]  20.8 us
    dot_general x1, matrix products, synthesize(): jnp.einsum('bkcf,kcn->bfn', spectra, window_table, preferred_element_type...  18.7 us
    add x1, other arithmetic, intersection_add(): intersection + jnp.pad(pieces_view[..., lag, :], leading + [(lag, pieces...  13.6 us
    another operation x1, local copies, waits for them, and re-layouts, beam_form(): return jnp.stack([real_part, imag_part], axis=2).astype(jnp.bfloat16)  11.4 us
  transfers between devices with their start and end apart: 3, of which 2 were waited for; matrix products, arithmetic and copies ran while one was open for 3% of the time, Pallas kernels for 0%

commit v1 on v0

v1 whole, which is shorter than its diff:
```python
import functools
import math

import jax
import jax.numpy as jnp
from jax import lax
from jax.experimental import pallas as pl
from jax.experimental.pallas import tpu as pltpu
from jax.sharding import PartitionSpec as P

M = 512
K = 256
FIRST_BIN = 32
GROUP = 4


def passed_along(block, axis, distance):
    devices = range(lax.axis_size(axis))
    route = [(i - distance, i) for i in devices if i - distance in devices]
    return lax.ppermute(block, axis, route)


def synth_table(prototype):
    length = prototype.shape[0]
    bin_index = jnp.arange(K, dtype=jnp.int32) + FIRST_BIN
    tap_index = jnp.arange(length, dtype=jnp.int32)
    phase_index = bin_index[:, None] * tap_index[None, :] % M
    angles = phase_index.astype(jnp.float32) * (2.0 * math.pi / M)
    scaled = prototype[None, :] / math.sqrt(K)
    window_table = jnp.stack([jnp.cos(angles) * scaled, -jnp.sin(angles) * scaled], axis=1)
    return window_table.astype(jnp.bfloat16)


def synth_kernel(*refs):
    *spectra_refs, table_ref, out_ref, tail_ref = refs
    hop = out_ref.shape[2]
    frames = out_ref.shape[1]
    lags = table_ref.shape[1] // hop
    rows = lax.broadcasted_iota(jnp.int32, (frames, hop), 0)
    for b in range(out_ref.shape[0]):
        columns = [r[:, b].reshape(-1, r.shape[3]) for r in spectra_refs]
        x = jnp.concatenate(columns, axis=0)
        y = lax.dot_general(
            x, table_ref[...], (((0,), (0,)), ((), ())), preferred_element_type=jnp.float32
        )
        main = y[:, :hop]
        tail = jnp.zeros((8, hop), jnp.float32)
        for lag in range(1, lags):
            turned = pltpu.roll(y[:, lag * hop : (lag + 1) * hop], lag, 0)
            main = main + jnp.where(rows >= lag, turned, 0.0)
            tail = tail + jnp.where(rows[:8] < lag, turned[:8], 0.0)
        out_ref[b] = main
        tail_ref[b] = tail


def synthesize(spectra, table, hop_size):
    groups, bands, beams, rows, frames = spectra.shape
    per_step = 2 if beams % 2 == 0 else 1
    specs = [
        pl.BlockSpec((None, bands, per_step, rows, frames), lambda i, g=g: (g, 0, i, 0, 0))
        for g in range(groups)
    ]
    flops = 2 * beams * frames * table.shape[0] * table.shape[1]
    return pl.pallas_call(
        synth_kernel,
        grid=(beams // per_step,),
        in_specs=specs + [pl.BlockSpec(table.shape, lambda i: (0, 0))],
        out_specs=[
            pl.BlockSpec((per_step, frames, hop_size), lambda i: (i, 0, 0)),
            pl.BlockSpec((per_step, 8, hop_size), lambda i: (i, 0, 0)),
        ],
        out_shape=[
            jax.ShapeDtypeStruct((beams, frames, hop_size), jnp.float32),
            jax.ShapeDtypeStruct((beams, 8, hop_size), jnp.float32),
        ],
        cost_estimate=pl.CostEstimate(flops=flops, bytes_accessed=20 << 20, transcendentals=0),
        compiler_params=pltpu.CompilerParams(vmem_limit_bytes=40 << 20),
    )(*([spectra] * groups), table)


def exchange_kernel(
    times, bands, samples_hbm, weights_hbm, out_hbm,
    samples, own, others, laid, sendbuf,
    load_sem, x_send, x_recv, b_send, b_recv,
):
    t = lax.axis_index("tm")
    band = lax.axis_index("band")
    groups = out_hbm.shape[0]
    beams = out_hbm.shape[2]
    width = own.shape[3]
    step = own.shape[0] // groups
    fan = width // beams
    tiles = laid.shape[0]

    barrier = pltpu.get_barrier_semaphore()

    @pl.loop(1, bands)
    def _(hop):
        pl.semaphore_signal(barrier, inc=1, device_id={"band": lax.rem(band + hop, bands)})

    for turn in range(1, times):
        pl.semaphore_signal(barrier, inc=1, device_id={"tm": lax.rem(t + turn, times)})
    pl.semaphore_wait(barrier, bands + times - 2)

    def weights_copy(g, turn):
        part = pl.ds(g * step, step)
        return pltpu.make_async_remote_copy(
            src_ref=weights_hbm.at[part],
            dst_ref=others.at[turn - 1, part],
            send_sem=x_send.at[turn - 1, g],
            recv_sem=x_recv.at[turn - 1, g],
            device_id={"tm": lax.rem(t + turn, times)},
        )

    def loads(g):
        part = pl.ds(g * step, step)
        return (
            pltpu.make_async_copy(samples_hbm.at[part], samples.at[part], load_sem.at[0, g]),
            pltpu.make_async_copy(weights_hbm.at[part], own.at[part], load_sem.at[1, g]),
        )

    for g in range(groups):
        for turn in range(1, times):
            weights_copy(g, turn).start()
    for g in range(groups):
        for copy in loads(g):
            copy.start()

    def spectra_copy(g, turn, i):
        first = lax.rem(t - turn + times, times) * fan
        return pltpu.make_async_remote_copy(
            src_ref=sendbuf.at[g, turn, pl.ds(i * beams, beams)],
            dst_ref=out_hbm.at[g, band],
            send_sem=b_send.at[g, turn, i],
            recv_sem=b_recv.at[g, band],
            device_id={"band": first + i},
        ), pltpu.make_async_copy(
            sendbuf.at[g, turn, pl.ds(i * beams, beams)],
            out_hbm.at[g, band],
            b_recv.at[g, band],
        ), first + i

    def contract(w, s):
        return lax.dot_general(
            w, s, (((0,), (1,)), ((), ())), preferred_element_type=jnp.float32
        )

    def form(g, turn):
        source = own if turn == 0 else others.at[turn - 1]

        @pl.loop(0, step)
        def _(kk):
            k = g * step + kk
            w0, w1 = source[k, 0], source[k, 1]
            s0, s1 = samples[k, 0], samples[k, 1]
            real_part = contract(w0, s0) + contract(w1, s1)
            imag_part = contract(w0, s1) - contract(w1, s0)
            for c, value in enumerate((real_part, imag_part)):
                for f in range(tiles):
                    laid[f, pl.ds(2 * kk + c, width, 2 * step), :] = value[:, f * 128 : (f + 1) * 128]

        for f in range(tiles):
            @pl.loop(0, fan)
            def _(i):
                rows = laid[f, pl.ds(i * beams * 2 * step, beams * 2 * step), :]
                sendbuf[g, turn, pl.ds(i * beams, beams), :, f * 128 : (f + 1) * 128] = (
                    rows.astype(jnp.bfloat16).reshape(beams, 2 * step, 128)
                )

        @pl.loop(0, fan)
        def _(i):
            remote, local, target = spectra_copy(g, turn, i)

            @pl.when(target == band)
            def _():
                local.start()

            @pl.when(target != band)
            def _():
                remote.start()

    @pl.loop(0, groups)
    def _(g):
        for copy in loads(g):
            copy.wait()
        form(g, 0)
        for turn in range(1, times):
            weights_copy(g, turn).wait_recv()
            form(g, turn)

    @pl.loop(0, groups)
    def _(g):
        for turn in range(1, times):
            weights_copy(g, turn).wait_send()
        for turn in range(times):
            @pl.loop(0, fan)
            def _(i):
                remote, _, target = spectra_copy(g, turn, i)

                @pl.when(target != band)
                def _():
                    remote.wait_send()

        @pl.loop(0, bands)
        def _(peer):
            pltpu.make_async_copy(
                out_hbm.at[g, peer], out_hbm.at[g, peer], b_recv.at[g, peer]
            ).wait()


def exchanged_spectra(samples, weights):
    times, bands = lax.axis_size("tm"), lax.axis_size("band")
    local, _, elements, width = weights.shape
    frames = samples.shape[2]
    step = math.gcd(GROUP, local)
    groups = local // step
    beams = width * times // bands
    tiles = frames // 128
    fan = width // beams
    flops = 8 * local * frames * elements * width * times
    return pl.pallas_call(
        functools.partial(exchange_kernel, times, bands),
        in_specs=[pl.BlockSpec(memory_space=pl.ANY)] * 2,
        out_specs=pl.BlockSpec(memory_space=pl.ANY),
        out_shape=jax.ShapeDtypeStruct((groups, bands, beams, 2 * step, frames), jnp.bfloat16),
        scratch_shapes=[
            pltpu.VMEM(samples.shape, jnp.bfloat16),
            pltpu.VMEM(weights.shape, jnp.bfloat16),
            pltpu.VMEM((times - 1,) + weights.shape, jnp.bfloat16),
            pltpu.VMEM((tiles, width * 2 * step, 128), jnp.float32),
            pltpu.VMEM((groups, times, width, 2 * step, frames), jnp.bfloat16),
            pltpu.SemaphoreType.DMA((2, groups)),
            pltpu.SemaphoreType.DMA((times - 1, groups)),
            pltpu.SemaphoreType.DMA((times - 1, groups)),
            pltpu.SemaphoreType.DMA((groups, times, fan)),
            pltpu.SemaphoreType.DMA((groups, bands)),
        ],
        cost_estimate=pl.CostEstimate(flops=flops, bytes_accessed=32 << 20, transcendentals=0),
        compiler_params=pltpu.CompilerParams(
            collective_id=0, has_side_effects=True, vmem_limit_bytes=56 << 20
        ),
    )(samples, weights)


def shards(samples, weights, prototype):
    hop_size = M // 2
    spectra = exchanged_spectra(samples.transpose(1, 2, 0, 3), weights)
    groups, bands, beams, rows, frame_total = spectra.shape
    length = prototype.shape[0]
    table = synth_table(prototype).reshape(bands, groups, rows, length)
    table = table.transpose(1, 0, 2, 3).reshape(K * 2, length)
    main, tail = synthesize(spectra, table, hop_size)
    prev_tail = passed_along(tail, "tm", 1)
    pad = jnp.pad(prev_tail, ((0, 0), (0, frame_total - 8), (0, 0)))
    return (main + pad).reshape(beams, frame_total * hop_size)


def solution(mesh):
    in_specs = (P("tm", "band", None, None), P("band", None, None, "tm"), P())
    out_specs = P("band", "tm")
    return jax.shard_map(shards, mesh=mesh, in_specs=in_specs, out_specs=out_specs, check_vma=False)
```

time: 553 us -> 290 us (0.52)
  waiting for transfers between devices: 376 us -> 12.4 us
  Pallas kernels: 0 us -> 248 us
  matrix products: 46.1 us -> 0 us
  local copies, waits for them, and re-layouts: 63 us -> 21.4 us
  other arithmetic: 43.4 us -> 6.32 us
  between operations: 13.5 us -> 0.07 us
  starting transfers between devices: 7.51 us -> 1.47 us
    pallas_call x0 -> x2, Pallas kernels: none -> 248 us  [the longest x1 232 us: exchanged_spectra(): pl.pallas_call(functools.partial(exchange_kernel, times, bands), in_specs...]
    all_gather x1 -> x0, waiting for transfers between devices: 199 us -> none  [shards(): lax.all_gather(weights, 'tm', axis=3, tiled=True)]
    all_to_all x1 -> x0, waiting for transfers between devices: 177 us -> none  [shards(): lax.all_to_all(beam_parts, 'band', split_axis=0, concat_axis=1, tiled=True)]
    dot_general x2 -> x0, matrix products: 46.1 us -> none  [the longest x1 27.4 us: beam_form(): jnp.einsum('fkce,kdeb->bkdcf', samples, weights, preferred_element_type=j...]
    add x3 -> x1, other arithmetic: 23.3 us -> 0.95 us  [shards(): return (main + pad).reshape(beams, frame_total * hop_size)]
    squeeze x1 -> x0, local copies, waits for them, and re-layouts: 20.8 us -> none  [intersection_add(): pieces_view[..., lag, :]]
    ppermute x1, waiting for transfers between devices: 0.01 us -> 12.4 us  [passed_along(): return lax.ppermute(block, axis, route)]
    another operation x1, local copies, waits for them, and re-layouts: 11.4 us -> 1.08 us  [synth_table(): jnp.stack([jnp.cos(angles) * scaled, -jnp.sin(angles) * scaled], axis=1)]
  transfers between devices with their start and end apart: 3 -> 1, of which waited for: 2 -> 1; matrix products, arithmetic and copies ran while one was open for 3% -> 0% of each run, Pallas kernels for 0% -> 0%
where the time goes in v1:
time: 290 us; the launch traced here: 289 us
  Pallas kernels  248 us (86%)
  local copies, waits for them, and re-layouts  21.4 us (7%)
  waiting for transfers between devices  12.4 us (4%)
  other arithmetic  6.32 us (2%)
    pallas_call x1, Pallas kernels, exchanged_spectra(): pl.pallas_call(functools.partial(exchange_kernel, times, bands), in_specs...  232 us
    unnamed x2, local copies, waits for them, and re-layouts  19.8 us
    pallas_call x1, Pallas kernels, synthesize(): pl.pallas_call(synth_kernel, grid=(beams // per_step,), in_specs=specs +...  15.7 us
    ppermute x1, waiting for transfers between devices, passed_along(): return lax.ppermute(block, axis, route)  12.4 us
  transfers between devices with their start and end apart: 1, of which 1 were waited for; matrix products, arithmetic and copies ran while one was open for 0% of the time, Pallas kernels for 0%

profile of v1, /device:TPU:14, one launch (start us, length us, event | category | flops | bytes accessed | tf_op | source)
XLA Modules:
  0.0 289.3 jit_solution(1564318440826875287)
XLA Ops:
  0.0 0.7 broadcast_multiply_fusion
  0.7 4.6 %multiply_convert_fusion.1 = (bf16[256,1,1024]{2,0,1:T(8,128)(2,1)S(1)}, bf16[256,1,1024]{2,0,1:T(8,128)(2,1)S(1)}) fusion(f32[1024]{0:T(1024)S(1)} %broadcast_multiply_fusion, s32[256]{0:T(256)S(1)} %iota_add_fusion), kind=kLoop, calls=%fused_computation.10 | loop fusion | flops 4980736 | bytes 1053696 | tf_op jit(solution)/shard_map/convert
  5.3 0.1 pad_maximum_fusion
  5.4 1.1 copy.8
  6.5 0.4 convert_element_type.24
  6.9 0.1 copy.9
  7.0 11.5 %copy.12 = bf16[256,16,2,512]{3,0,2,1:T(8,128)(2,1)} copy(bf16[256,16,2,512]{3,2,1,0:T(2,128)(2,1)} %param.3) | data formatting | bytes 16777216 | tf_op args[0]
  18.5 231.9 %shard_map.37.refs_0_.refs_1_.refs_2_.refs_3_ = bf16[4,16,32,8,256]{4,3,2,1,0:T(8,128)(2,1)} custom-call(bf16[16,2,256,512]{3,2,1,0:T(8,128)(2,1)} %bitcast.9, bf16[16,2,512,256]{3,2,1,0:T(8,128)(2,1)} %weights_hbm.1), custom_call_target="tpu_custom_call" | custom-call | flops 8589934592 | bytes 33554432 | tf_op jit(solution)/shard_map/pallas_call | solution.py:221
  250.5 15.7 %shard_map.38 = (f32[32,256,256]{2,1,0:T(8,128)S(1)}, f32[32,8,256]{2,1,0:T(8,128)S(1)}) custom-call(bf16[4,16,32,8,256]{4,3,2,1,0:T(8,128)(2,1)} %shard_map.37.refs_0_.refs_1_.refs_2_.refs_3_, bf16[4,16,32,8,256]{4,3,2,1,0:T(8,128)(2,1)} %shard_map.37.refs_0_.refs_1_.refs_2_.refs_3_, bf16[4,16,32,8,256]{4,3,2,1,0:T(8,128)(2,1)} %shard_map.37.refs_0_.refs_1_.refs_2_.refs_3_, ...), custom_call_target="tpu_custom_call" | custom-call | flops 8589934592 | bytes 20971520 | tf_op jit(solution)/shard_map/pallas_call | solution.py:64
  266.1 1.5 collective-permute-start
  267.6 12.4 %collective-permute-done = f32[32,8,256]{2,1,0:T(8,128)S(1)} collective-permute-done((f32[32,8,256]{2,1,0:T(8,128)S(1)}, f32[32,8,256]{2,1,0:T(8,128)S(1)}, u32[]{:S(2)}, u32[]{:S(2)}) %collective-permute-start) | collective-permute-done | bytes 262176 | tf_op jit(solution)/shard_map/ppermute | solution.py:20
  280.0 0.9 pad_add_fusion
  281.0 8.3 %copy.10 = f32[4,8,256,256]{3,1,2,0:T(8,128)} copy(f32[4,8,256,256]{3,2,1,0:T(8,128)S(1)} %bitcast.8) | data formatting | bytes 16777216
  (1 shorter events, 0.0 us)
Async XLA Ops:
  266.1 13.9 %collective-permute-start = (f32[32,8,256]{2,1,0:T(8,128)S(1)}, f32[32,8,256]{2,1,0:T(8,128)S(1)}, u32[]{:S(2)}, u32[]{:S(2)}) collective-permute-start(f32[32,8,256]{2,1,0:T(8,128)S(1)} %get-tuple-element.8), channel_id=1, source_target_pairs={{0,16},{1,17},{2,18},{3,19},{4,20},{5,21},{6,22},{7,23},{8,24},{9,... | collective-permute-start | bytes 786440 | tf_op jit(solution)/shard_map/ppermute | solution.py:20

commit v2 on v1

--- a/solution.py
+++ b/solution.py
@@ -11,7 +11,9 @@
 M = 512
 K = 256
 FIRST_BIN = 32
-GROUP = 4
+GROUP = 1
+LANES = 128
+SUBLANES = 8
 
 
 def passed_along(block, axis, distance):
@@ -20,24 +22,15 @@
     return lax.ppermute(block, axis, route)
 
 
-def synth_table(prototype):
-    length = prototype.shape[0]
-    bin_index = jnp.arange(K, dtype=jnp.int32) + FIRST_BIN
-    tap_index = jnp.arange(length, dtype=jnp.int32)
-    phase_index = bin_index[:, None] * tap_index[None, :] % M
-    angles = phase_index.astype(jnp.float32) * (2.0 * math.pi / M)
-    scaled = prototype[None, :] / math.sqrt(K)
-    window_table = jnp.stack([jnp.cos(angles) * scaled, -jnp.sin(angles) * scaled], axis=1)
-    return window_table.astype(jnp.bfloat16)
-
-
 def synth_kernel(*refs):
     *spectra_refs, table_ref, out_ref, tail_ref = refs
-    hop = out_ref.shape[2]
-    frames = out_ref.shape[1]
+    hop = tail_ref.shape[2]
+    frames = spectra_refs[0].shape[3]
     lags = table_ref.shape[1] // hop
+    pieces = hop // LANES
+    per_step = tail_ref.shape[0]
     rows = lax.broadcasted_iota(jnp.int32, (frames, hop), 0)
-    for b in range(out_ref.shape[0]):
+    for b in range(per_step):
         columns = [r[:, b].reshape(-1, r.shape[3]) for r in spectra_refs]
         x = jnp.concatenate(columns, axis=0)
         y = lax.dot_general(
@@ -49,38 +42,46 @@
             turned = pltpu.roll(y[:, lag * hop : (lag + 1) * hop], lag, 0)
             main = main + jnp.where(rows >= lag, turned, 0.0)
             tail = tail + jnp.where(rows[:8] < lag, turned[:8], 0.0)
-        out_ref[b] = main
+        slot = pl.program_id(1) * per_step + b
+        for m in range(pieces):
+            out_ref[pl.ds(m * SUBLANES + slot, frames, pieces * SUBLANES), :] = (
+                main[:, m * LANES : (m + 1) * LANES]
+            )
         tail_ref[b] = tail
 
 
 def synthesize(spectra, table, hop_size):
     groups, bands, beams, rows, frames = spectra.shape
-    per_step = 2 if beams % 2 == 0 else 1
+    per_step = 2
+    inner = SUBLANES // per_step
+    tile_rows = frames * hop_size // LANES * SUBLANES
     specs = [
-        pl.BlockSpec((None, bands, per_step, rows, frames), lambda i, g=g: (g, 0, i, 0, 0))
+        pl.BlockSpec(
+            (None, bands, per_step, rows, frames), lambda i, j, g=g: (g, 0, i * inner + j, 0, 0)
+        )
         for g in range(groups)
     ]
     flops = 2 * beams * frames * table.shape[0] * table.shape[1]
     return pl.pallas_call(
         synth_kernel,
-        grid=(beams // per_step,),
-        in_specs=specs + [pl.BlockSpec(table.shape, lambda i: (0, 0))],
+        grid=(beams // SUBLANES, inner),
+        in_specs=specs + [pl.BlockSpec(table.shape, lambda i, j: (0, 0))],
         out_specs=[
-            pl.BlockSpec((per_step, frames, hop_size), lambda i: (i, 0, 0)),
-            pl.BlockSpec((per_step, 8, hop_size), lambda i: (i, 0, 0)),
+            pl.BlockSpec((tile_rows, LANES), lambda i, j: (i, 0)),
+            pl.BlockSpec((per_step, 8, hop_size), lambda i, j: (i * inner + j, 0, 0)),
         ],
         out_shape=[
-            jax.ShapeDtypeStruct((beams, frames, hop_size), jnp.float32),
+            jax.ShapeDtypeStruct((beams // SUBLANES * tile_rows, LANES), jnp.float32),
             jax.ShapeDtypeStruct((beams, 8, hop_size), jnp.float32),
         ],
         cost_estimate=pl.CostEstimate(flops=flops, bytes_accessed=20 << 20, transcendentals=0),
-        compiler_params=pltpu.CompilerParams(vmem_limit_bytes=40 << 20),
+        compiler_params=pltpu.CompilerParams(vmem_limit_bytes=60 << 20),
     )(*([spectra] * groups), table)
 
 
 def exchange_kernel(
-    times, bands, samples_hbm, weights_hbm, out_hbm,
-    samples, own, others, laid, sendbuf,
+    times, bands, samples_hbm, weights_hbm, prototype_ref, out_hbm, table_ref,
+    raw, wide, samples, own, others, laid, sendbuf,
     load_sem, x_send, x_recv, b_send, b_recv,
 ):
     t = lax.axis_index("tm")
@@ -115,7 +116,7 @@
     def loads(g):
         part = pl.ds(g * step, step)
         return (
-            pltpu.make_async_copy(samples_hbm.at[part], samples.at[part], load_sem.at[0, g]),
+            pltpu.make_async_copy(samples_hbm.at[:, part], raw.at[:, part], load_sem.at[0, g]),
             pltpu.make_async_copy(weights_hbm.at[part], own.at[part], load_sem.at[1, g]),
         )
 
@@ -152,19 +153,19 @@
         def _(kk):
             k = g * step + kk
             w0, w1 = source[k, 0], source[k, 1]
-            s0, s1 = samples[k, 0], samples[k, 1]
+            s0, s1 = samples[kk, 0], samples[kk, 1]
             real_part = contract(w0, s0) + contract(w1, s1)
             imag_part = contract(w0, s1) - contract(w1, s0)
             for c, value in enumerate((real_part, imag_part)):
                 for f in range(tiles):
-                    laid[f, pl.ds(2 * kk + c, width, 2 * step), :] = value[:, f * 128 : (f + 1) * 128]
+                    laid[f, pl.ds(2 * kk + c, width, 2 * step), :] = value[:, f * LANES : (f + 1) * LANES]
 
         for f in range(tiles):
             @pl.loop(0, fan)
             def _(i):
                 rows = laid[f, pl.ds(i * beams * 2 * step, beams * 2 * step), :]
-                sendbuf[g, turn, pl.ds(i * beams, beams), :, f * 128 : (f + 1) * 128] = (
-                    rows.astype(jnp.bfloat16).reshape(beams, 2 * step, 128)
+                sendbuf[g, turn, pl.ds(i * beams, beams), :, f * LANES : (f + 1) * LANES] = (
+                    rows.astype(jnp.bfloat16).reshape(beams, 2 * step, LANES)
                 )
 
         @pl.loop(0, fan)
@@ -178,12 +179,39 @@
             @pl.when(target != band)
             def _():
                 remote.start()
+
+    frames = raw.shape[0]
+    packed = raw.shape[2]
+
+    def separate(g):
+        @pl.loop(0, step)
+        def _(kk):
+            wide[...] = raw[:, g * step + kk].astype(jnp.float32).reshape(frames * packed, LANES)
+            for piece in range(packed // 2):
+                for c in range(2):
+                    plane = wide[pl.ds(2 * piece + c, frames, packed), :]
+                    samples[kk, c, :, piece * LANES : (piece + 1) * LANES] = plane.astype(jnp.bfloat16)
+
+    def tabulate(g):
+        rows = table_ref.shape[0] // groups
+        length = table_ref.shape[1]
+        row = lax.broadcasted_iota(jnp.int32, (rows, length), 0)
+        tap = lax.broadcasted_iota(jnp.int32, (rows, length), 1)
+        part = row // 2
+        subband = (part // step) * (step * groups) + g * step + lax.rem(part, step) + FIRST_BIN
+        phase = lax.rem(subband * tap + lax.rem(row, 2) * (M // 4), M)
+        scaled = jnp.cos(phase.astype(jnp.float32) * (2.0 * math.pi / M)) * (
+            prototype_ref[...] / math.sqrt(K)
+        )
+        table_ref[pl.ds(pl.multiple_of(g * rows, rows), rows), :] = scaled.astype(jnp.bfloat16)
 
     @pl.loop(0, groups)
     def _(g):
         for copy in loads(g):
             copy.wait()
+        separate(g)
         form(g, 0)
+        tabulate(g)
         for turn in range(1, times):
             weights_copy(g, turn).wait_recv()
             form(g, turn)
@@ -208,26 +236,31 @@
             ).wait()
 
 
-def exchanged_spectra(samples, weights):
+def exchanged_spectra(samples, weights, prototype):
     times, bands = lax.axis_size("tm"), lax.axis_size("band")
     local, _, elements, width = weights.shape
-    frames = samples.shape[2]
+    frames, _, packed, _ = samples.shape
     step = math.gcd(GROUP, local)
     groups = local // step
     beams = width * times // bands
-    tiles = frames // 128
+    tiles = frames // LANES
     fan = width // beams
     flops = 8 * local * frames * elements * width * times
     return pl.pallas_call(
         functools.partial(exchange_kernel, times, bands),
-        in_specs=[pl.BlockSpec(memory_space=pl.ANY)] * 2,
-        out_specs=pl.BlockSpec(memory_space=pl.ANY),
-        out_shape=jax.ShapeDtypeStruct((groups, bands, beams, 2 * step, frames), jnp.bfloat16),
+        in_specs=[pl.BlockSpec(memory_space=pl.ANY)] * 2 + [pl.BlockSpec(memory_space=pltpu.VMEM)],
+        out_specs=[pl.BlockSpec(memory_space=pl.ANY), pl.BlockSpec(memory_space=pltpu.VMEM)],
+        out_shape=[
+            jax.ShapeDtypeStruct((groups, bands, beams, 2 * step, frames), jnp.bfloat16),
+            jax.ShapeDtypeStruct((2 * local * bands, prototype.shape[1]), jnp.bfloat16),
+        ],
         scratch_shapes=[
             pltpu.VMEM(samples.shape, jnp.bfloat16),
+            pltpu.VMEM((frames * packed, LANES), jnp.float32),
+            pltpu.VMEM((step, 2, frames, elements), jnp.bfloat16),
             pltpu.VMEM(weights.shape, jnp.bfloat16),
             pltpu.VMEM((times - 1,) + weights.shape, jnp.bfloat16),
-            pltpu.VMEM((tiles, width * 2 * step, 128), jnp.float32),
+            pltpu.VMEM((tiles, width * 2 * step, LANES), jnp.float32),
             pltpu.VMEM((groups, times, width, 2 * step, frames), jnp.bfloat16),
             pltpu.SemaphoreType.DMA((2, groups)),
             pltpu.SemaphoreType.DMA((times - 1, groups)),
@@ -239,20 +272,23 @@
         compiler_params=pltpu.CompilerParams(
             collective_id=0, has_side_effects=True, vmem_limit_bytes=56 << 20
         ),
-    )(samples, weights)
+    )(samples, weights, prototype)
 
 
 def shards(samples, weights, prototype):
     hop_size = M // 2
-    spectra = exchanged_spectra(samples.transpose(1, 2, 0, 3), weights)
-    groups, bands, beams, rows, frame_total = spectra.shape
-    length = prototype.shape[0]
-    table = synth_table(prototype).reshape(bands, groups, rows, length)
-    table = table.transpose(1, 0, 2, 3).reshape(K * 2, length)
-    main, tail = synthesize(spectra, table, hop_size)
-    prev_tail = passed_along(tail, "tm", 1)
-    pad = jnp.pad(prev_tail, ((0, 0), (0, frame_total - 8), (0, 0)))
-    return (main + pad).reshape(beams, frame_total * hop_size)
+    frames, local, _, elements = samples.shape
+    pieces = elements // LANES
+    packed = samples.reshape(frames, local, 2, pieces, LANES).transpose(0, 1, 3, 2, 4)
+    packed = packed.reshape(frames, local, 2 * pieces, LANES)
+    spectra, table = exchanged_spectra(packed, weights, prototype[None, :])
+    beams = spectra.shape[2]
+    tiles, tail = synthesize(spectra, table, hop_size)
+    prev_tail = passed_along(tail, "tm", 1).reshape(beams, -1)
+    series = tiles.reshape(beams // SUBLANES, frames * hop_size // LANES, SUBLANES, LANES)
+    series = series.transpose(0, 2, 1, 3).reshape(beams, frames * hop_size)
+    head = series[:, : prev_tail.shape[1]] + prev_tail
+    return lax.dynamic_update_slice(series, head, (0, 0))
 
 
 def solution(mesh):

time: 290 us -> 239 us (0.82)
  Pallas kernels: 248 us -> 225 us
  local copies, waits for them, and re-layouts: 21.4 us -> 0.08 us
  other arithmetic: 6.32 us -> 1.7 us
  waiting for transfers between devices: 12.4 us -> 9.43 us
    pallas_call x1, Pallas kernels: 232 us -> 204 us  [exchanged_spectra(): pl.pallas_call(functools.partial(exchange_kernel, times, bands), in_specs...]
    unnamed x2 -> x1, local copies, waits for them, and re-layouts: 19.8 us -> 0.08 us
    pallas_call x1, Pallas kernels: 15.7 us -> 20.9 us  [synthesize(): pl.pallas_call(synth_kernel, grid=(beams // SUBLANES, inner), in_specs=sp...]
    another operation x2 -> x0, other arithmetic: 4.68 us -> none
    ppermute x1, waiting for transfers between devices: 12.4 us -> 9.43 us  [passed_along(): return lax.ppermute(block, axis, route)]
where the time goes in v2:
time: 239 us; the launch traced here: 238 us
  Pallas kernels  225 us (94%)
  waiting for transfers between devices  9.43 us (4%)
    pallas_call x1, Pallas kernels, exchanged_spectra(): pl.pallas_call(functools.partial(exchange_kernel, times, bands), in_specs...  204 us
    pallas_call x1, Pallas kernels, synthesize(): pl.pallas_call(synth_kernel, grid=(beams // SUBLANES, inner), in_specs=sp...  20.9 us
    ppermute x1, waiting for transfers between devices, passed_along(): return lax.ppermute(block, axis, route)  9.43 us
  transfers between devices with their start and end apart: 1, of which 1 were waited for; matrix products, arithmetic and copies ran while one was open for 0% of the time, Pallas kernels for 0%

profile of v2, /device:TPU:14, one launch (start us, length us, event | category | flops | bytes accessed | tf_op | source)
XLA Modules:
  0.0 237.8 jit_solution(9624365527944058032)
XLA Ops:
  0.0 204.4 %shard_map.37 = (bf16[16,16,32,2,256]{4,3,2,1,0:T(2,128)(2,1)}, bf16[512,1024]{1,0:T(8,128)(2,1)}) custom-call(bf16[256,16,8,128]{3,2,1,0:T(8,128)(2,1)} %bitcast.16, bf16[16,2,512,256]{3,2,1,0:T(8,128)(2,1)} %weights_hbm.1, f32[1,1024]{1,0:T(1,128)} %bitcast.17), custom_call_target="tpu_custom_call" | custom-call | flops 8589934592 | bytes 33554432 | tf_op jit(solution)/shard_map/pallas_call | solution.py:249
  204.4 20.9 %shard_map.38 = (f32[16384,128]{1,0:T(8,128)}, f32[32,8,256]{2,1,0:T(8,128)}) custom-call(bf16[16,16,32,2,256]{4,3,2,1,0:T(2,128)(2,1)} %get-tuple-element.9.refs_0_.refs_1_.refs_2_.refs_3_.refs_4_.refs_5_.refs_6_.refs_7_.refs_8_.refs_9_.refs_10_.refs_11_.refs_12_.refs_13_.refs_14_.refs_15_, ...), custom_call_target="tpu_custom_call" | custom-call | flops 8589934592 | bytes 20971520 | tf_op jit(solution)/shard_map/pallas_call | solution.py:65
  225.3 1.3 collective-permute-start
  226.6 9.4 %collective-permute-done = f32[32,8,256]{2,1,0:T(8,128)S(1)} collective-permute-done((f32[32,8,256]{2,1,0:T(8,128)}, f32[32,8,256]{2,1,0:T(8,128)S(1)}, u32[]{:S(2)}, u32[]{:S(2)}) %collective-permute-start) | collective-permute-done | bytes 262176 | tf_op jit(solution)/shard_map/ppermute | solution.py:22
  236.1 0.1 copy.5
  236.1 1.7 fusion
Async XLA Ops:
  225.3 10.7 %collective-permute-start = (f32[32,8,256]{2,1,0:T(8,128)}, f32[32,8,256]{2,1,0:T(8,128)S(1)}, u32[]{:S(2)}, u32[]{:S(2)}) collective-permute-start(f32[32,8,256]{2,1,0:T(8,128)} %get-tuple-element.12), channel_id=1, source_target_pairs={{0,16},{1,17},{2,18},{3,19},{4,20},{5,21},{6,22},{7,23},{8,24},{9,... | collective-permute-start | bytes 786440 | tf_op jit(solution)/shard_map/ppermute | solution.py:22

commit v3 on v2

--- a/solution.py
+++ b/solution.py
@@ -52,7 +52,7 @@
 
 def synthesize(spectra, table, hop_size):
     groups, bands, beams, rows, frames = spectra.shape
-    per_step = 2
+    per_step = 8
     inner = SUBLANES // per_step
     tile_rows = frames * hop_size // LANES * SUBLANES
     specs = [

time: 239 us -> 233 us (0.975)
  Pallas kernels: 225 us -> 220 us
    pallas_call x1, Pallas kernels: 20.9 us -> 15.5 us  [synthesize(): pl.pallas_call(synth_kernel, grid=(beams // SUBLANES, inner), in_specs=sp...]
where the time goes in v3:
time: 233 us; the launch traced here: 232 us
  Pallas kernels  220 us (94%)
  waiting for transfers between devices  9.44 us (4%)
    pallas_call x1, Pallas kernels, exchanged_spectra(): pl.pallas_call(functools.partial(exchange_kernel, times, bands), in_specs...  204 us
    pallas_call x1, Pallas kernels, synthesize(): pl.pallas_call(synth_kernel, grid=(beams // SUBLANES, inner), in_specs=sp...  15.5 us
    ppermute x1, waiting for transfers between devices, passed_along(): return lax.ppermute(block, axis, route)  9.44 us
  transfers between devices with their start and end apart: 1, of which 1 were waited for; matrix products, arithmetic and copies ran while one was open for 0% of the time, Pallas kernels for 0%

profile of v3, /device:TPU:14, one launch (start us, length us, event | category | flops | bytes accessed | tf_op | source)
XLA Modules:
  0.0 232.4 jit_solution(10612753635452178872)
XLA Ops:
  0.0 204.4 %shard_map.37 = (bf16[16,16,32,2,256]{4,3,2,1,0:T(2,128)(2,1)}, bf16[512,1024]{1,0:T(8,128)(2,1)}) custom-call(bf16[256,16,8,128]{3,2,1,0:T(8,128)(2,1)} %bitcast.16, bf16[16,2,512,256]{3,2,1,0:T(8,128)(2,1)} %weights_hbm.1, f32[1,1024]{1,0:T(1,128)} %bitcast.17), custom_call_target="tpu_custom_call" | custom-call | flops 8589934592 | bytes 33554432 | tf_op jit(solution)/shard_map/pallas_call | solution.py:249
  204.4 15.5 %shard_map.38 = (f32[16384,128]{1,0:T(8,128)}, f32[32,8,256]{2,1,0:T(8,128)}) custom-call(bf16[16,16,32,2,256]{4,3,2,1,0:T(2,128)(2,1)} %get-tuple-element.9.refs_0_.refs_1_.refs_2_.refs_3_.refs_4_.refs_5_.refs_6_.refs_7_.refs_8_.refs_9_.refs_10_.refs_11_.refs_12_.refs_13_.refs_14_.refs_15_, ...), custom_call_target="tpu_custom_call" | custom-call | flops 8589934592 | bytes 20971520 | tf_op jit(solution)/shard_map/pallas_call | solution.py:65
  219.9 1.3 collective-permute-start
  221.2 9.4 %collective-permute-done = f32[32,8,256]{2,1,0:T(8,128)S(1)} collective-permute-done((f32[32,8,256]{2,1,0:T(8,128)}, f32[32,8,256]{2,1,0:T(8,128)S(1)}, u32[]{:S(2)}, u32[]{:S(2)}) %collective-permute-start) | collective-permute-done | bytes 262176 | tf_op jit(solution)/shard_map/ppermute | solution.py:22
  230.6 0.1 copy.5
  230.7 1.7 fusion
Async XLA Ops:
  219.9 10.7 %collective-permute-start = (f32[32,8,256]{2,1,0:T(8,128)}, f32[32,8,256]{2,1,0:T(8,128)S(1)}, u32[]{:S(2)}, u32[]{:S(2)}) collective-permute-start(f32[32,8,256]{2,1,0:T(8,128)} %get-tuple-element.12), channel_id=1, source_target_pairs={{0,16},{1,17},{2,18},{3,19},{4,20},{5,21},{6,22},{7,23},{8,24},{9,... | collective-permute-start | bytes 786440 | tf_op jit(solution)/shard_map/ppermute | solution.py:22
